TPU v7x, 32 devices: a whole 2x2x4 slice. The times are simulated.
32 devices in a mesh: tile: 8 (over z, x), freq: 4 (over y, core).
Axes of the slice: x: 2, y: 2, z: 4, core: 2. Of those that a mesh axis runs over, the one named last changes fastest.
Arguments:
- u_tiles: bfloat16 [4, 8, 8, 40, 1024], P('freq', 'tile'), may hold values from -0.3125 to 0.3125
- v_tiles: bfloat16 [4, 8, 8, 40, 1024], P('freq', None, 'tile'), may hold values from -0.1875 to 0.1875
- tile_ranks: int32 [4, 8, 8], P('freq'), may hold values from 4 to 40, as said below
- recorded: float32 [4, 8192, 128], P('freq', 'tile')
Outputs:
- model: float32 [4, 8192, 128], P('freq', 'tile')
- residual: float32 [4, 8192, 128], P('freq', 'tile')
- gradient: float32 [4, 8192, 128], P('freq', 'tile')
Inputs may be any that keep to these rules, and one draw needn't show every extreme that they name: `tile_ranks`: every draw holds a tile of rank 40 and a tile of rank 4.
All inputs are finite; a program needn't handle non-finite values.
Results may differ from a plain program's by a relative error of at most 0.02.
Values may be sent and summed in bfloat16 or wider, within the bound.
No kernel may reach another device: no remote copies, remote signals or barrier semaphores. Data moves between devices by JAX's collectives and lax.ppermute only.
A program may use at most 128 MiB of HBM per device.

v0:
```python
import jax
import jax.numpy as jnp
from jax import lax
from jax.sharding import PartitionSpec as P

ITERS = 2


def local(u_tiles, v_tiles, tile_ranks, recorded):
    count_freq, tile_dev, tiles_all, rank_pad, width = u_tiles.shape
    traces = recorded.shape[2]
    position = lax.axis_index("tile")
    levels = jnp.arange(rank_pad, dtype=jnp.int32)
    rank_rows = lax.dynamic_slice_in_dim(tile_ranks, position * tile_dev, tile_dev, 1)
    rank_cols = lax.dynamic_slice_in_dim(tile_ranks, position * tile_dev, tile_dev, 2)
    mask_rows = (levels < rank_rows[..., None]).astype(jnp.float32)[..., None]
    mask_cols = (levels < rank_cols[..., None]).astype(jnp.float32)[..., None]

    def apply_cols_part(coeffs):
        return jnp.einsum("fijrb,fijrs->fjbs", v_tiles, coeffs, preferred_element_type=jnp.float32)

    def column_coeffs(rounded):
        coeffs = jnp.einsum(
            "fijrb,fjbs->fijrs", v_tiles, rounded, preferred_element_type=jnp.float32
        )
        return (coeffs * mask_cols).astype(jnp.bfloat16)

    def row_coeffs(rounded):
        coeffs = jnp.einsum(
            "fijrb,fibs->fijrs", u_tiles, rounded, preferred_element_type=jnp.float32
        )
        return (coeffs * mask_rows).astype(jnp.bfloat16)

    def adjoint(field):
        rounded = field.astype(jnp.bfloat16).reshape(count_freq, tile_dev, width, traces)
        coeffs = row_coeffs(rounded)
        image = apply_cols_part(
            lax.all_to_all(coeffs, "tile", split_axis=2, concat_axis=1, tiled=True)
        )
        return image.reshape(count_freq, tile_dev * width, traces)

    def squares(field):
        return lax.psum(jnp.sum(field * field), ("tile", "freq"))

    model = jnp.zeros_like(recorded)
    resid = recorded
    gradient = adjoint(resid)
    direction = gradient
    gamma = squares(gradient)
    for iteration in range(ITERS):
        forward_rounded = direction.astype(jnp.bfloat16).reshape(
            count_freq, tile_dev, width, traces
        )
        forward_coeffs = column_coeffs(forward_rounded)
        forward_image = jnp.einsum(
            "fijrb,fijrs->fibs",
            u_tiles,
            lax.all_to_all(forward_coeffs, "tile", split_axis=1, concat_axis=2, tiled=True),
            preferred_element_type=jnp.float32,
        )
        image = forward_image.reshape(count_freq, tile_dev * width, traces)
        delta = squares(image)
        alpha = gamma / delta
        model = model + alpha * direction
        resid = resid - alpha * image
        gradient = adjoint(resid)
        gamma_new = squares(gradient)
        direction = gradient + gamma_new / gamma * direction
        gamma = gamma_new
    return (model, resid, gradient)


def solution(mesh):
    placed = (
        P("freq", "tile", None, None, None),
        P("freq", None, "tile", None, None),
        P("freq", None, None),
        P("freq", "tile", None),
    )
    return jax.shard_map(
        local,
        mesh=mesh,
        in_specs=placed,
        out_specs=(P("freq", "tile", None), P("freq", "tile", None), P("freq", "tile", None)),
        check_vma=False,
    )
```

profile of v0, /device:TPU:0, one launch (start us, length us, event | category | flops | bytes accessed | tf_op | source)
XLA Modules:
  0.0 193.8 jit_solution(4762774457426976636)
XLA Ops:
  0.6 0.0 copy-start
  0.6 0.0 copy-start.4
  0.7 0.7 copy-done.4
  1.4 0.1 fusion.37
  1.5 2.2 %fusion.9 = bf16[1,1,8,40,128]{4,3,1,0,2:T(8,128)(2,1)} fusion(bf16[1,1,8,40,1024]{4,3,2,1,0:T(8,128)(2,1)} %param.4, f32[1,1024,128]{2,1,0:T(8,128)} %param.7, f32[8,40]{1,0:T(8,128)S(1)} %fusion.37), kind=kOutput, calls=%fused_computation.19 | convolution fusion | flops 84099072 | bytes 1262848 | tf_op jit(solution)/shard_map/fijrb,fibs->fijrs/dot_general | solution.py:29
  3.7 7.3 %all-to-all-start = ((bf16[1,1,8,40,128]{4,3,1,0,2:T(8,128)(2,1)}), bf16[1,1,8,40,128]{4,3,1,0,2:T(8,128)(2,1)S(1)}, u32[]{:S(2)}, u32[]{:S(2)}) async-start(bf16[1,1,8,40,128]{4,3,1,0,2:T(8,128)(2,1)} %fusion.9), calls=%async_computation | async-start | bytes 163840 | tf_op jit(solution)/shard_map/all_to_all | solution.py:38
  11.0 0.2 dynamic-slice_reduce_fusion
  11.2 0.1 fusion.38
  11.2 6.8 %all-to-all-done = bf16[1,1,8,40,128]{4,3,1,0,2:T(8,128)(2,1)S(1)} async-done(((bf16[1,1,8,40,128]{4,3,1,0,2:T(8,128)(2,1)}), bf16[1,1,8,40,128]{4,3,1,0,2:T(8,128)(2,1)S(1)}, u32[]{:S(2)}, u32[]{:S(2)}) %all-to-all-start) | async-done | bytes 81952 | tf_op jit(solution)/shard_map/all_to_all | solution.py:38
  18.0 0.0 copy-done
  18.0 1.0 multiply_reduce_fusion.3
  19.0 0.0 copy-start.3
  19.0 1.0 fusion.10
  20.0 0.0 copy-start.1
  20.0 3.5 %all-to-all-start.1 = ((bf16[1,8,1,40,128]{4,3,2,0,1:T(8,128)(2,1)}), bf16[1,8,1,40,128]{4,3,2,0,1:T(8,128)(2,1)S(1)}, u32[]{:S(2)}, u32[]{:S(2)}) async-start(bf16[1,8,1,40,128]{4,3,2,0,1:T(8,128)(2,1)} %fusion.10), calls=%async_computation.1 | async-start | bytes 163840 | tf_op jit(solution)/shard_map/all_to_all | solution.py:58
  23.5 0.0 copy-done.3
  23.5 0.2 copy.15
  23.7 6.7 %all-to-all-done.1 = bf16[1,8,1,40,128]{4,3,2,0,1:T(8,128)(2,1)S(1)} async-done(((bf16[1,8,1,40,128]{4,3,2,0,1:T(8,128)(2,1)}), bf16[1,8,1,40,128]{4,3,2,0,1:T(8,128)(2,1)S(1)}, u32[]{:S(2)}, u32[]{:S(2)}) %all-to-all-start.1) | async-done | bytes 81952 | tf_op jit(solution)/shard_map/all_to_all | solution.py:58
  30.4 0.0 copy-done.1
  30.4 1.0 multiply_reduce_fusion.2
  31.4 0.0 copy-start.2
  31.4 38.6 %all-reduce = (f32[]{:T(128)}, f32[]{:T(128)}) all-reduce(f32[]{:T(128)} %get-tuple-element.11, f32[]{:T(128)} %get-tuple-element.13), channel_id=1, replica_groups=mesh['tile'=8,'freq'=4] {'tile','freq'}, use_global_device_ids=true, to_apply=%region_1.0 | all-reduce | flops 2 | bytes 16 | tf_op jit(solution)/shard_map/psum | solution.py:43
  71.4 0.4 fusion.8
  71.7 0.0 copy-done.2
  71.8 11.3 %all_to_all.20 = bf16[1,1,8,40,128]{4,3,1,0,2:T(8,128)(2,1)S(1)} all-to-all(bf16[1,1,8,40,128]{4,3,1,0,2:T(8,128)(2,1)S(1)} %fusion.8), channel_id=1, replica_groups=mesh['tile'=8,'freq'=4] {'tile'}, dimensions={2} | all-to-all | bytes 163840 | tf_op jit(solution)/shard_map/all_to_all | solution.py:38
  83.1 1.0 multiply_reduce_fusion.1
  84.1 38.6 %psum.30 = f32[]{:T(128)} all-reduce(f32[]{:T(128)} %get-tuple-element.15), channel_id=1, replica_groups=mesh['tile'=8,'freq'=4] {'tile','freq'}, use_global_device_ids=true, to_apply=%region_5.0 | all-reduce | flops 1 | bytes 8 | tf_op jit(solution)/shard_map/psum | solution.py:43
  124.1 0.4 fusion.11
  124.5 11.3 %all_to_all.21 = bf16[1,8,1,40,128]{4,3,2,0,1:T(8,128)(2,1)S(1)} all-to-all(bf16[1,8,1,40,128]{4,3,2,0,1:T(8,128)(2,1)S(1)} %fusion.11), channel_id=1, replica_groups=mesh['tile'=8,'freq'=4] {'tile'}, dimensions={1} | all-to-all | bytes 163840 | tf_op jit(solution)/shard_map/all_to_all | solution.py:58
  135.8 1.7 multiply_reduce_fusion
  137.5 38.7 %psum.31 = f32[]{:T(128)} all-reduce(f32[]{:T(128)} %get-tuple-element.17), channel_id=1, replica_groups=mesh['tile'=8,'freq'=4] {'tile','freq'}, use_global_device_ids=true, to_apply=%region_7.0 | all-reduce | flops 1 | bytes 8 | tf_op jit(solution)/shard_map/psum | solution.py:43
  177.6 1.3 bitcast_subtract_fusion
  179.0 1.0 fusion.7
  179.9 1.0 copy.22
  180.9 4.5 %all-to-all-start.4 = ((bf16[1,1,8,40,128]{4,3,1,0,2:T(8,128)(2,1)}), bf16[1,1,8,40,128]{4,3,1,0,2:T(8,128)(2,1)S(1)}, u32[]{:S(2)}, u32[]{:S(2)}) async-start(bf16[1,1,8,40,128]{4,3,1,0,2:T(8,128)(2,1)} %fusion.7), calls=%async_computation.4 | async-start | bytes 163840 | tf_op jit(solution)/shard_map/all_to_all | solution.py:38
  185.5 0.1 add_bitcast_fusion
  185.6 1.0 copy.21
  186.6 5.9 %all-to-all-done.4 = bf16[1,1,8,40,128]{4,3,1,0,2:T(8,128)(2,1)S(1)} async-done(((bf16[1,1,8,40,128]{4,3,1,0,2:T(8,128)(2,1)}), bf16[1,1,8,40,128]{4,3,1,0,2:T(8,128)(2,1)S(1)}, u32[]{:S(2)}, u32[]{:S(2)}) %all-to-all-start.4) | async-done | bytes 81952 | tf_op jit(solution)/shard_map/all_to_all | solution.py:38
  192.5 0.3 convolution_bitcast_fusion
  192.8 1.0 copy.23
  (1 shorter events, 0.0 us)
Async XLA Ops:
  0.6 17.4 %copy-start = (bf16[1,8,1,40,1024]{4,3,2,1,0:T(8,128)(2,1)S(1)}, bf16[1,8,1,40,1024]{4,3,2,1,0:T(8,128)(2,1)}, u32[]{:S(2)}) copy-start(bf16[1,8,1,40,1024]{4,3,2,1,0:T(8,128)(2,1)} %param.5) | copy-start | bytes 1966084
  0.6 0.8 copy-start.4
  3.7 14.3 %all-to-all-start = ((bf16[1,1,8,40,128]{4,3,1,0,2:T(8,128)(2,1)}), bf16[1,1,8,40,128]{4,3,1,0,2:T(8,128)(2,1)S(1)}, u32[]{:S(2)}, u32[]{:S(2)}) async-start(bf16[1,1,8,40,128]{4,3,1,0,2:T(8,128)(2,1)} %fusion.9), calls=%async_computation | async-start | bytes 163840 | tf_op jit(solution)/shard_map/all_to_all | solution.py:38
  19.0 4.5 %copy-start.3 = (f32[1,1024,128]{2,1,0:T(8,128)S(1)}, f32[1,1024,128]{2,1,0:T(8,128)}, u32[]{:S(2)}) copy-start(f32[1,1024,128]{2,1,0:T(8,128)} %param.7) | copy-start | bytes 1572868
  20.0 10.5 %copy-start.1 = (bf16[1,1,8,40,1024]{4,3,2,1,0:T(8,128)(2,1)S(1)}, bf16[1,1,8,40,1024]{4,3,2,1,0:T(8,128)(2,1)}, u32[]{:S(2)}) copy-start(bf16[1,1,8,40,1024]{4,3,2,1,0:T(8,128)(2,1)} %param.4) | copy-start | bytes 1966084
  20.0 10.4 %all-to-all-start.1 = ((bf16[1,8,1,40,128]{4,3,2,0,1:T(8,128)(2,1)}), bf16[1,8,1,40,128]{4,3,2,0,1:T(8,128)(2,1)S(1)}, u32[]{:S(2)}, u32[]{:S(2)}) async-start(bf16[1,8,1,40,128]{4,3,2,0,1:T(8,128)(2,1)} %fusion.10), calls=%async_computation.1 | async-start | bytes 163840 | tf_op jit(solution)/shard_map/all_to_all | solution.py:58
  31.4 40.3 %copy-start.2 = (f32[128,1024]{1,0:T(8,128)}, f32[128,1024]{1,0:T(8,128)S(1)}, u32[]{:S(2)}) copy-start(f32[128,1024]{1,0:T(8,128)S(1)} %get-tuple-element.14) | copy-start | bytes 1572868
  180.9 11.6 %all-to-all-start.4 = ((bf16[1,1,8,40,128]{4,3,1,0,2:T(8,128)(2,1)}), bf16[1,1,8,40,128]{4,3,1,0,2:T(8,128)(2,1)S(1)}, u32[]{:S(2)}, u32[]{:S(2)}) async-start(bf16[1,1,8,40,128]{4,3,1,0,2:T(8,128)(2,1)} %fusion.7), calls=%async_computation.4 | async-start | bytes 163840 | tf_op jit(solution)/shard_map/all_to_all | solution.py:38
where the time goes:
time: 195 us; the launch traced here: 194 us
  blocking collectives  139 us (71%)
  waiting for transfers between devices  19.4 us (10%)
  starting transfers between devices  15.3 us (8%)
  matrix products  9.88 us (5%)
  between operations  4.83 us (2%)
  local copies, waits for them, and re-layouts  4.13 us (2%)
    psum x3, blocking collectives, squares(): return lax.psum(jnp.sum(field * field), ('tile', 'freq'))  116 us
    all_to_all x2, waiting for transfers between devices, adjoint(): lax.all_to_all(coeffs, 'tile', split_axis=2, concat_axis=1, tiled=True)  12.7 us
    all_to_all x2, starting transfers between devices, adjoint(): lax.all_to_all(coeffs, 'tile', split_axis=2, concat_axis=1, tiled=True)  11.8 us
    all_to_all x1, blocking collectives, adjoint(): lax.all_to_all(coeffs, 'tile', split_axis=2, concat_axis=1, tiled=True)  11.3 us
    all_to_all x1, blocking collectives, local(): lax.all_to_all(forward_coeffs, 'tile', split_axis=1, concat_axis=2, tiled...  11.3 us
    all_to_all x1, waiting for transfers between devices, local(): lax.all_to_all(forward_coeffs, 'tile', split_axis=1, concat_axis=2, tiled...  6.74 us
    unnamed x14, local copies, waits for them, and re-layouts  3.95 us
  transfers between devices with their start and end apart: 3, of which 3 were waited for; matrix products, arithmetic and copies ran while one was open for 1% of the time, Pallas kernels for 0%

commit v1 on v0

--- a/solution.py
+++ b/solution.py
@@ -35,7 +35,12 @@
         rounded = field.astype(jnp.bfloat16).reshape(count_freq, tile_dev, width, traces)
         coeffs = row_coeffs(rounded)
         image = apply_cols_part(
-            lax.all_to_all(coeffs, "tile", split_axis=2, concat_axis=1, tiled=True)
+            jnp.concatenate(
+                lax.all_to_all(
+                    jnp.stack(jnp.split(coeffs, lax.axis_size("tile"), axis=2)), "tile", 0, 0
+                ),
+                axis=1,
+            )
         )
         return image.reshape(count_freq, tile_dev * width, traces)
 

time: 195 us -> 203 us (1.041)
  local copies, waits for them, and re-layouts: 4.13 us -> 13.8 us
    unnamed x14 -> x35, local copies, waits for them, and re-layouts: 3.95 us -> 12.4 us
where the time goes in v1:
time: 203 us; the launch traced here: 202 us
  blocking collectives  139 us (68%)
  waiting for transfers between devices  19.4 us (10%)
  starting transfers between devices  15.3 us (8%)
  local copies, waits for them, and re-layouts  13.8 us (7%)
  matrix products  8.62 us (4%)
  between operations  4.88 us (2%)
    psum x3, blocking collectives, squares(): return lax.psum(jnp.sum(field * field), ('tile', 'freq'))  116 us
    all_to_all x2, waiting for transfers between devices, adjoint(): lax.all_to_all(jnp.stack(jnp.split(coeffs, lax.axis_size('tile'), axis=2)...  12.7 us
    unnamed x35, local copies, waits for them, and re-layouts  12.4 us
    all_to_all x2, starting transfers between devices, adjoint(): lax.all_to_all(jnp.stack(jnp.split(coeffs, lax.axis_size('tile'), axis=2)...  11.8 us
    all_to_all x1, blocking collectives, local(): lax.all_to_all(forward_coeffs, 'tile', split_axis=1, concat_axis=2, tiled...  11.3 us
    all_to_all x1, blocking collectives, adjoint(): lax.all_to_all(jnp.stack(jnp.split(coeffs, lax.axis_size('tile'), axis=2)...  11.3 us
    all_to_all x1, waiting for transfers between devices, local(): lax.all_to_all(forward_coeffs, 'tile', split_axis=1, concat_axis=2, tiled...  6.74 us
  transfers between devices with their start and end apart: 3, of which 3 were waited for; matrix products, arithmetic and copies ran while one was open for 1% of the time, Pallas kernels for 0%

profile of v1, /device:TPU:0, one launch (start us, length us, event | category | flops | bytes accessed | tf_op | source)
XLA Modules:
  0.0 202.3 jit_solution(17460094858374889610)
XLA Ops:
  0.6 0.0 copy-start
  0.6 0.0 copy-start.4
  0.7 0.7 copy-done.4
  1.4 0.1 fusion.37
  1.5 1.6 fusion.9
  3.1 0.6 constant_dynamic-update-slice_fusion.7
  3.7 0.6 constant_dynamic-update-slice_fusion.6
  4.3 0.6 constant_dynamic-update-slice_fusion.5
  4.9 0.6 constant_dynamic-update-slice_fusion.4
  5.5 0.6 constant_dynamic-update-slice_fusion.3
  6.1 0.6 constant_dynamic-update-slice_fusion.2
  6.7 0.6 constant_dynamic-update-slice_fusion.1
  7.3 0.6 constant_dynamic-update-slice_fusion
  7.9 7.3 %all-to-all-start = ((bf16[8,1,1,1,40,128]{5,4,3,2,1,0:T(8,128)(2,1)}), bf16[8,1,1,1,40,128]{5,4,3,2,1,0:T(8,128)(2,1)S(1)}, u32[]{:S(2)}, u32[]{:S(2)}) async-start(bf16[8,1,1,1,40,128]{5,4,3,2,1,0:T(8,128)(2,1)} %constant_dynamic-update-slice_fusion), calls=%async_computation | async-start | bytes 163840 | tf_op jit(solution)/shard_map/all_to_all | solution.py:39
  15.1 0.2 dynamic-slice_reduce_fusion
  15.3 0.1 fusion.38
  15.4 6.8 %all-to-all-done = bf16[8,1,1,1,40,128]{5,4,3,2,1,0:T(8,128)(2,1)S(1)} async-done(((bf16[8,1,1,1,40,128]{5,4,3,2,1,0:T(8,128)(2,1)}), bf16[8,1,1,1,40,128]{5,4,3,2,1,0:T(8,128)(2,1)S(1)}, u32[]{:S(2)}, u32[]{:S(2)}) %all-to-all-start) | async-done | bytes 81952 | tf_op jit(solution)/shard_map/all_to_all | solution.py:39
  22.2 0.0 copy-done
  22.2 1.0 multiply_reduce_fusion.3
  23.2 0.0 copy-start.3
  23.2 1.0 fusion.10
  24.1 0.0 copy-start.1
  24.1 3.5 %all-to-all-start.1 = ((bf16[1,8,1,40,128]{4,3,2,0,1:T(8,128)(2,1)}), bf16[1,8,1,40,128]{4,3,2,0,1:T(8,128)(2,1)S(1)}, u32[]{:S(2)}, u32[]{:S(2)}) async-start(bf16[1,8,1,40,128]{4,3,2,0,1:T(8,128)(2,1)} %fusion.10), calls=%async_computation.1 | async-start | bytes 163840 | tf_op jit(solution)/shard_map/all_to_all | solution.py:63
  27.6 0.0 copy-done.3
  27.6 0.2 copy.14
  27.9 6.7 %all-to-all-done.1 = bf16[1,8,1,40,128]{4,3,2,0,1:T(8,128)(2,1)S(1)} async-done(((bf16[1,8,1,40,128]{4,3,2,0,1:T(8,128)(2,1)}), bf16[1,8,1,40,128]{4,3,2,0,1:T(8,128)(2,1)S(1)}, u32[]{:S(2)}, u32[]{:S(2)}) %all-to-all-start.1) | async-done | bytes 81952 | tf_op jit(solution)/shard_map/all_to_all | solution.py:63
  34.6 0.0 copy-done.1
  34.6 1.0 multiply_reduce_fusion.2
  35.6 0.0 copy-start.2
  35.6 38.6 %all-reduce = (f32[]{:T(128)}, f32[]{:T(128)}) all-reduce(f32[]{:T(128)} %get-tuple-element.11, f32[]{:T(128)} %get-tuple-element.13), channel_id=1, replica_groups=mesh['tile'=8,'freq'=4] {'tile','freq'}, use_global_device_ids=true, to_apply=%region_1.0 | all-reduce | flops 2 | bytes 16 | tf_op jit(solution)/shard_map/psum | solution.py:48
  75.6 0.4 fusion.8
  75.9 0.0 copy-done.2
  76.0 11.3 %all_to_all.33 = bf16[8,1,1,1,40,128]{5,4,3,2,1,0:T(8,128)(2,1)S(1)} all-to-all(bf16[8,1,1,1,40,128]{5,4,3,2,1,0:T(8,128)(2,1)S(1)} %constant_dynamic-update-slice_fusion.8), channel_id=1, replica_groups=mesh['tile'=8,'freq'=4] {'tile'}, dimensions={0} | all-to-all | bytes 163840 | tf_op jit(solution)/shard_map/all_to_all | solution.py:39
  87.4 1.0 multiply_reduce_fusion.1
  88.4 38.6 %psum.30 = f32[]{:T(128)} all-reduce(f32[]{:T(128)} %get-tuple-element.15), channel_id=1, replica_groups=mesh['tile'=8,'freq'=4] {'tile','freq'}, use_global_device_ids=true, to_apply=%region_5.0 | all-reduce | flops 1 | bytes 8 | tf_op jit(solution)/shard_map/psum | solution.py:48
  128.4 0.4 fusion.11
  128.7 11.3 %all_to_all.34 = bf16[1,8,1,40,128]{4,3,2,0,1:T(8,128)(2,1)S(1)} all-to-all(bf16[1,8,1,40,128]{4,3,2,0,1:T(8,128)(2,1)S(1)} %fusion.11), channel_id=1, replica_groups=mesh['tile'=8,'freq'=4] {'tile'}, dimensions={1} | all-to-all | bytes 163840 | tf_op jit(solution)/shard_map/all_to_all | solution.py:63
  140.1 1.7 multiply_reduce_fusion
  141.8 38.7 %psum.31 = f32[]{:T(128)} all-reduce(f32[]{:T(128)} %get-tuple-element.17), channel_id=1, replica_groups=mesh['tile'=8,'freq'=4] {'tile','freq'}, use_global_device_ids=true, to_apply=%region_7.0 | all-reduce | flops 1 | bytes 8 | tf_op jit(solution)/shard_map/psum | solution.py:48
  181.9 1.3 bitcast_subtract_fusion
  183.2 0.4 fusion.7
  183.6 1.0 copy.19
  184.6 0.6 constant_dynamic-update-slice_fusion.23
  185.2 0.6 constant_dynamic-update-slice_fusion.22
  185.8 0.6 constant_dynamic-update-slice_fusion.21
  186.4 0.6 constant_dynamic-update-slice_fusion.20
  187.0 0.6 constant_dynamic-update-slice_fusion.19
  187.6 0.6 constant_dynamic-update-slice_fusion.18
  188.2 0.6 constant_dynamic-update-slice_fusion.17
  188.8 0.6 constant_dynamic-update-slice_fusion.16
  189.4 4.5 %all-to-all-start.4 = ((bf16[8,1,1,1,40,128]{5,4,3,2,1,0:T(8,128)(2,1)}), bf16[8,1,1,1,40,128]{5,4,3,2,1,0:T(8,128)(2,1)S(1)}, u32[]{:S(2)}, u32[]{:S(2)}) async-start(bf16[8,1,1,1,40,128]{5,4,3,2,1,0:T(8,128)(2,1)} %constant_dynamic-update-slice_fusion.16), calls=%async_computation.4 | async-start | bytes 163840 | tf_op jit(solution)/shard_map/all_to_all | solution.py:39
  193.9 0.1 add_bitcast_fusion
  194.0 1.0 copy.18
  195.0 5.9 %all-to-all-done.4 = bf16[8,1,1,1,40,128]{5,4,3,2,1,0:T(8,128)(2,1)S(1)} async-done(((bf16[8,1,1,1,40,128]{5,4,3,2,1,0:T(8,128)(2,1)}), bf16[8,1,1,1,40,128]{5,4,3,2,1,0:T(8,128)(2,1)S(1)}, u32[]{:S(2)}, u32[]{:S(2)}) %all-to-all-start.4) | async-done | bytes 81952 | tf_op jit(solution)/shard_map/all_to_all | solution.py:39
  200.9 0.3 convolution_bitcast_fusion
  201.3 1.0 copy.20
  (9 shorter events, 0.1 us)
Async XLA Ops:
  0.6 21.5 %copy-start = (bf16[1,8,1,40,1024]{4,3,2,1,0:T(8,128)(2,1)S(1)}, bf16[1,8,1,40,1024]{4,3,2,1,0:T(8,128)(2,1)}, u32[]{:S(2)}) copy-start(bf16[1,8,1,40,1024]{4,3,2,1,0:T(8,128)(2,1)} %param.5) | copy-start | bytes 1966084
  0.6 0.8 copy-start.4
  7.9 14.3 %all-to-all-start = ((bf16[8,1,1,1,40,128]{5,4,3,2,1,0:T(8,128)(2,1)}), bf16[8,1,1,1,40,128]{5,4,3,2,1,0:T(8,128)(2,1)S(1)}, u32[]{:S(2)}, u32[]{:S(2)}) async-start(bf16[8,1,1,1,40,128]{5,4,3,2,1,0:T(8,128)(2,1)} %constant_dynamic-update-slice_fusion), calls=%async_computation | async-start | bytes 163840 | tf_op jit(solution)/shard_map/all_to_all | solution.py:39
  23.2 4.5 %copy-start.3 = (f32[1,1024,128]{2,1,0:T(8,128)S(1)}, f32[1,1024,128]{2,1,0:T(8,128)}, u32[]{:S(2)}) copy-start(f32[1,1024,128]{2,1,0:T(8,128)} %param.7) | copy-start | bytes 1572868
  24.1 10.5 %copy-start.1 = (bf16[1,1,8,40,1024]{4,3,2,1,0:T(8,128)(2,1)S(1)}, bf16[1,1,8,40,1024]{4,3,2,1,0:T(8,128)(2,1)}, u32[]{:S(2)}) copy-start(bf16[1,1,8,40,1024]{4,3,2,1,0:T(8,128)(2,1)} %param.4) | copy-start | bytes 1966084
  24.1 10.4 %all-to-all-start.1 = ((bf16[1,8,1,40,128]{4,3,2,0,1:T(8,128)(2,1)}), bf16[1,8,1,40,128]{4,3,2,0,1:T(8,128)(2,1)S(1)}, u32[]{:S(2)}, u32[]{:S(2)}) async-start(bf16[1,8,1,40,128]{4,3,2,0,1:T(8,128)(2,1)} %fusion.10), calls=%async_computation.1 | async-start | bytes 163840 | tf_op jit(solution)/shard_map/all_to_all | solution.py:63
  35.6 40.3 %copy-start.2 = (f32[128,1024]{1,0:T(8,128)}, f32[128,1024]{1,0:T(8,128)S(1)}, u32[]{:S(2)}) copy-start(f32[128,1024]{1,0:T(8,128)S(1)} %get-tuple-element.14) | copy-start | bytes 1572868
  189.4 11.6 %all-to-all-start.4 = ((bf16[8,1,1,1,40,128]{5,4,3,2,1,0:T(8,128)(2,1)}), bf16[8,1,1,1,40,128]{5,4,3,2,1,0:T(8,128)(2,1)S(1)}, u32[]{:S(2)}, u32[]{:S(2)}) async-start(bf16[8,1,1,1,40,128]{5,4,3,2,1,0:T(8,128)(2,1)} %constant_dynamic-update-slice_fusion.16), calls=%async_computation.4 | async-start | bytes 163840 | tf_op jit(solution)/shard_map/all_to_all | solution.py:39
